TPU v7x, 32 devices: a whole 2x2x4 slice. The times are simulated.
32 devices in a mesh: dp: 2 (over y), table: 16 (over z, x, core).
Axes of the slice: x: 2, y: 2, z: 4, core: 2. Of those that a mesh axis runs over, the one named last changes fastest.
Arguments:
- gradients: bfloat16 [256, 4096], P(None, ('dp', 'table')), may hold values from -16 to 16
- row_ids: int32 [4096], P(('dp', 'table')), may hold values from 0 to 32767
- table_block: float32 [256, 32768], P('table', 'dp'), may hold values from -6 to 6
- adagrad_state: float32 [32768], P('dp'), may hold values from 0.05 to 2
Outputs:
- new_table: float32 [256, 32768], P('table', 'dp')
- new_state: float32 [32768], P('dp')
All inputs are finite; a program needn't handle non-finite values.
Results may differ from a plain program's by a relative error of at most 0.0003.
Values may be sent and summed in bfloat16 or wider, within the bound.
A program may use at most 64 MiB of HBM per device.

v0:
```python
import jax
import jax.numpy as jnp
from jax import lax
from jax.sharding import PartitionSpec as P

W = 256
learn_rate = 0.5


def accumulate(grads, ids, first_row, count_rows):
    relative = ids - first_row
    inside = (relative >= 0) & (relative < count_rows)
    target = jnp.where(inside, relative, count_rows)
    start_total = jnp.zeros((grads.shape[0], count_rows), jnp.float32)
    return start_total.at[:, target].add(grads.astype(jnp.float32), mode="drop")


def body(gradients, row_ids, table_block, adagrad_state):
    owned = lax.all_to_all(gradients, "table", split_axis=0, concat_axis=1, tiled=True)
    local_rows = table_block.shape[1]
    all_row_ids = lax.all_gather(row_ids, ("dp", "table"), axis=0, tiled=True)
    first_row = lax.axis_index("dp") * local_rows
    row_grad = accumulate(
        lax.all_gather(owned, "dp", axis=1, tiled=True), all_row_ids, first_row, local_rows
    )
    partial_squares = jnp.sum(row_grad * row_grad, axis=0)
    squares = lax.psum(partial_squares, "table")
    new_state = adagrad_state + squares / W
    new_table = table_block - learn_rate * row_grad / jnp.sqrt(new_state)[None, :]
    return (new_table, new_state)


def solution(mesh):
    in_specs = (P(None, ("dp", "table")), P(("dp", "table")), P("table", "dp"), P("dp"))
    out_specs = (P("table", "dp"), P("dp"))
    return jax.shard_map(body, mesh=mesh, in_specs=in_specs, out_specs=out_specs, check_vma=False)
```

profile of v0, /device:TPU:8, one launch (start us, length us, event | category | flops | bytes accessed | tf_op | source)
XLA Modules:
  0.0 214.5 jit_solution(18062439507933522561)
XLA Ops:
  7.2 6.3 %all-to-all-start = ((bf16[16,16,128]{2,1,0:T(8,128)(2,1)}), bf16[16,16,128]{2,1,0:T(8,128)(2,1)S(1)}, u32[]{:S(2)}, u32[]{:S(2)}) async-start(bf16[16,16,128]{2,1,0:T(8,128)(2,1)} %bitcast.12), calls=%async_computation | async-start | bytes 131072 | tf_op jit(solution)/shard_map/all_to_all | solution.py:19
  13.4 0.0 all-reduce.2.cloned.1.call-start
  13.5 38.0 %all-gather = s32[32,1,128]{2,1,0:T(1,128)S(1)} all-gather(s32[1,1,128]{2,1,0:T(1,128)} %bitcast.15), channel_id=1, replica_groups=mesh['dp'=2,'table'=16] {'dp','table'}, dimensions={0}, use_global_device_ids=true | all-gather | bytes 16896 | tf_op jit(solution)/shard_map/all_gather | solution.py:21
  51.5 0.0 all-to-all-done
  51.5 0.3 copy.9
  51.8 14.8 %all_gather.7 = bf16[16,4096]{0,1:T(8,128)(2,1)S(1)} all-gather(bf16[16,2048]{0,1:T(8,128)(2,1)S(1)} %bitcast.10), channel_id=1, replica_groups=mesh['dp'=2,'table'=16] {'dp'}, dimensions={1}, use_global_device_ids=true | all-gather | bytes 196608 | tf_op jit(solution)/shard_map/all_gather | solution.py:24
  66.7 0.0 copy-start
  66.7 26.1 %scatter_custom_fusion = f32[16,16384]{0,1:T(8,128)} fusion(s32[4096]{0:T(1024)S(1)} %compare_select_fusion, f32[]{:T(128)} %constant.7.clone.1, bf16[16,4096]{0,1:T(8,128)(2,1)S(1)} %all_gather.7), kind=kCustom, calls=%fused_computation.3 | custom fusion | flops 131072 | bytes 2097156 | tf_op jit(solution)/shard_map/scatter-add | solution.py:15
  92.8 0.0 copy-start.1
  92.8 5.3 %multiply_reduce_fusion = f32[16384]{0:T(1024)} fusion(f32[16,16384]{0,1:T(8,128)} %scatter_custom_fusion), kind=kLoop, calls=%fused_computation.2 | loop fusion | flops 507904 | bytes 1114112 | tf_op jit(solution)/shard_map/reduce_sum | solution.py:26
  98.1 0.0 all-reduce.2.cloned.1.call-update
  98.1 0.0 copy-done
  98.1 4.6 %copy.10 = f32[16,16384]{0,1:T(8,128)} copy(f32[16,16384]{1,0:T(8,128)S(1)} %copy-done) | data formatting | bytes 2097152 | tf_op args[2]
  102.7 84.2 %all-reduce.2.cloned.1.call-done = f32[16384]{0:T(1024)} async-done(((f32[16384]{0:T(1024)}), f32[16384]{0:T(1024)}) %all-reduce.2.cloned.1.call-update) | async-done | bytes 65552 | tf_op jit(solution)/shard_map/psum | solution.py:27
  186.9 0.0 copy-done.1
  186.9 1.5 fusion.4
  188.4 13.3 %divide_subtract_fusion = f32[16,16384]{0,1:T(8,128)} fusion(f32[16,16384]{0,1:T(8,128)} %copy.10, f32[16,16384]{0,1:T(8,128)} %scatter_custom_fusion, f32[16384]{0:T(1024)S(1)} %get-tuple-element.6), kind=kLoop, calls=%fused_computation.1 | loop fusion | flops 786432 | bytes 3211264 | tf_op jit(solution)/shard_map/sub | solution.py:29
  201.7 6.0 %copy.11 = f32[16,16384]{1,0:T(8,128)} copy(f32[16,16384]{0,1:T(8,128)} %divide_subtract_fusion) | data formatting | bytes 2097152
  (2 shorter events, 0.0 us)
Async XLA Ops:
  7.2 44.4 %all-to-all-start = ((bf16[16,16,128]{2,1,0:T(8,128)(2,1)}), bf16[16,16,128]{2,1,0:T(8,128)(2,1)S(1)}, u32[]{:S(2)}, u32[]{:S(2)}) async-start(bf16[16,16,128]{2,1,0:T(8,128)(2,1)} %bitcast.12), calls=%async_computation | async-start | bytes 131072 | tf_op jit(solution)/shard_map/all_to_all | solution.py:19
  13.4 173.5 %all-reduce.2.cloned.1.call-start = ((), (), s32[]{:S(2)}) async-start(), calls=%async_computation.1 | async-start | bytes 131072 | tf_op jit(solution)/shard_map/psum | solution.py:27
  66.7 31.4 %copy-start = (f32[16,16384]{1,0:T(8,128)S(1)}, f32[16,16384]{1,0:T(8,128)}, u32[]{:S(2)}) copy-start(f32[16,16384]{1,0:T(8,128)} %param.6) | copy-start | bytes 3145732
  92.8 94.1 %copy-start.1 = (f32[16384]{0:T(1024)S(1)}, f32[16384]{0:T(1024)}, u32[]{:S(2)}) copy-start(f32[16384]{0:T(1024)} %param.7) | copy-start | bytes 196612
Sparse Core Ops, SparseCore 0:
  98.2 88.6 all-reduce.1
where the time goes:
time: 215 us
  waiting for transfers between devices  84.2 us (39%)
  blocking collectives  52.9 us (25%)
  other arithmetic  46.2 us (21%)
  between operations  14.1 us (7%)
  local copies, waits for them, and re-layouts  10.9 us (5%)
  starting transfers between devices  6.32 us (3%)
    psum x1, waiting for transfers between devices, body(): squares = lax.psum(partial_squares, 'table')  84.2 us
    all_gather x1, blocking collectives, body(): all_row_ids = lax.all_gather(row_ids, ('dp', 'table'), axis=0, tiled=True)  38 us
    scatter-add x1, other arithmetic, accumulate(): return start_total.at[:, target].add(grads.astype(jnp.float32), mode='drop')  26.1 us
    all_gather x1, blocking collectives, body(): lax.all_gather(owned, 'dp', axis=1, tiled=True)  14.8 us
    sub x1, other arithmetic, body(): table_block - learn_rate * row_grad / jnp.sqrt(new_state)[None, :]  13.3 us
    unnamed x6, local copies, waits for them, and re-layouts  10.6 us
    all_to_all x1, starting transfers between devices, body(): lax.all_to_all(gradients, 'table', split_axis=0, concat_axis=1, tiled=True)  6.28 us
    reduce_sum x1, other arithmetic, body(): partial_squares = jnp.sum(row_grad * row_grad, axis=0)  5.28 us
  transfers between devices with their start and end apart: 2, of which 1 were waited for; matrix products, arithmetic and copies ran while one was open for 2% of the time, Pallas kernels for 0%

commit v1 on v0

--- a/solution.py
+++ b/solution.py
@@ -24,7 +24,7 @@
         lax.all_gather(owned, "dp", axis=1, tiled=True), all_row_ids, first_row, local_rows
     )
     partial_squares = jnp.sum(row_grad * row_grad, axis=0)
-    squares = lax.psum(partial_squares, "table")
+    squares = lax.all_gather(partial_squares, axis_name="table").sum(axis=0)
     new_state = adagrad_state + squares / W
     new_table = table_block - learn_rate * row_grad / jnp.sqrt(new_state)[None, :]
     return (new_table, new_state)

time: 215 us -> 166 us (0.77); the launches traced: 215 us -> 163 us
  waiting for transfers between devices: 84.2 us -> 32.2 us
    psum x1 -> x0, waiting for transfers between devices: 84.2 us -> none  [body(): squares = lax.psum(partial_squares, 'table')]
    all_gather x0 -> x1, waiting for transfers between devices: none -> 32.2 us  [body(): squares = lax.all_gather(partial_squares, axis_name='table').sum(axis=0)]
  transfers between devices with their start and end apart: 2 -> 2, of which waited for: 1 -> 1; matrix products, arithmetic and copies ran while one was open for 2% -> 3% of each run, Pallas kernels for 0% -> 0%
where the time goes in v1:
time: 166 us; the launch traced here: 163 us
  blocking collectives  52.9 us (32%)
  other arithmetic  45.5 us (27%)
  waiting for transfers between devices  32.2 us (19%)
  between operations  14.1 us (8%)
  local copies, waits for them, and re-layouts  12.3 us (7%)
  starting transfers between devices  6.32 us (4%)
    all_gather x1, blocking collectives, body(): all_row_ids = lax.all_gather(row_ids, ('dp', 'table'), axis=0, tiled=True)  38 us
    all_gather x1, waiting for transfers between devices, body(): squares = lax.all_gather(partial_squares, axis_name='table').sum(axis=0)  32.2 us
    scatter-add x1, other arithmetic, accumulate(): return start_total.at[:, target].add(grads.astype(jnp.float32), mode='drop')  26.1 us
    all_gather x1, blocking collectives, body(): lax.all_gather(owned, 'dp', axis=1, tiled=True)  14.8 us
    sub x1, other arithmetic, body(): table_block - learn_rate * row_grad / jnp.sqrt(new_state)[None, :]  13.3 us
    unnamed x6, local copies, waits for them, and re-layouts  10.6 us
    all_to_all x1, starting transfers between devices, body(): lax.all_to_all(gradients, 'table', split_axis=0, concat_axis=1, tiled=True)  6.28 us
    reduce_sum x1, other arithmetic, body(): partial_squares = jnp.sum(row_grad * row_grad, axis=0)  5.25 us
  transfers between devices with their start and end apart: 2, of which 1 were waited for; matrix products, arithmetic and copies ran while one was open for 3% of the time, Pallas kernels for 0%

profile of v1, /device:TPU:8, one launch (start us, length us, event | category | flops | bytes accessed | tf_op | source)
XLA Modules:
  0.0 163.3 jit_solution(18394290371067912784)
XLA Ops:
  7.2 6.3 %all-to-all-start = ((bf16[16,16,128]{2,1,0:T(8,128)(2,1)}), bf16[16,16,128]{2,1,0:T(8,128)(2,1)S(1)}, u32[]{:S(2)}, u32[]{:S(2)}) async-start(bf16[16,16,128]{2,1,0:T(8,128)(2,1)} %bitcast.12), calls=%async_computation | async-start | bytes 131072 | tf_op jit(solution)/shard_map/all_to_all | solution.py:19
  13.4 0.0 all-gather.4.cloned.1.call-start
  13.5 38.0 %all-gather.1 = s32[32,1,128]{2,1,0:T(1,128)S(1)} all-gather(s32[1,1,128]{2,1,0:T(1,128)} %bitcast.15), channel_id=1, replica_groups=mesh['dp'=2,'table'=16] {'dp','table'}, dimensions={0}, use_global_device_ids=true | all-gather | bytes 16896 | tf_op jit(solution)/shard_map/all_gather | solution.py:21
  51.5 0.0 all-to-all-done
  51.5 0.3 copy.12
  51.8 14.8 %all_gather.13 = bf16[16,4096]{0,1:T(8,128)(2,1)S(1)} all-gather(bf16[16,2048]{0,1:T(8,128)(2,1)S(1)} %bitcast.10), channel_id=1, replica_groups=mesh['dp'=2,'table'=16] {'dp'}, dimensions={1}, use_global_device_ids=true | all-gather | bytes 196608 | tf_op jit(solution)/shard_map/all_gather | solution.py:24
  66.7 0.0 copy-start
  66.7 26.1 %scatter_custom_fusion = f32[16,16384]{0,1:T(8,128)} fusion(s32[4096]{0:T(1024)S(1)} %compare_select_fusion, f32[]{:T(128)} %constant.7.clone.1, bf16[16,4096]{0,1:T(8,128)(2,1)S(1)} %all_gather.13), kind=kCustom, calls=%fused_computation.3 | custom fusion | flops 131072 | bytes 2097156 | tf_op jit(solution)/shard_map/scatter-add | solution.py:15
  92.8 5.3 %multiply_reduce_fusion = f32[16384]{0:T(1024)} fusion(f32[16,16384]{0,1:T(8,128)} %scatter_custom_fusion), kind=kLoop, calls=%fused_computation.2 | loop fusion | flops 507904 | bytes 1114112 | tf_op jit(solution)/shard_map/reduce_sum | solution.py:26
  98.0 0.0 copy-start.1
  98.0 0.0 all-gather.4.cloned.1.call-update
  98.1 0.0 copy-done
  98.1 4.6 %copy.13 = f32[16,16384]{0,1:T(8,128)} copy(f32[16,16384]{1,0:T(8,128)S(1)} %copy-done) | data formatting | bytes 2097152 | tf_op args[2]
  102.7 32.2 %all-gather.4.cloned.1.call-done = f32[262144]{0:T(1024)} async-done(((f32[16384]{0:T(1024)}), f32[262144]{0:T(1024)}) %all-gather.4.cloned.1.call-update) | async-done | bytes 1048592 | tf_op jit(solution)/shard_map/all_gather | solution.py:27
  134.9 1.4 reshape.16
  136.4 0.2 reduce_sum.19
  136.5 0.0 copy-done.1
  136.5 0.6 fusion.4
  137.2 13.3 %divide_subtract_fusion = f32[16,16384]{0,1:T(8,128)} fusion(f32[16,16384]{0,1:T(8,128)} %copy.13, f32[16,16384]{0,1:T(8,128)} %scatter_custom_fusion, f32[16384]{0:T(1024)S(1)} %get-tuple-element.8), kind=kLoop, calls=%fused_computation.1 | loop fusion | flops 786432 | bytes 3211264 | tf_op jit(solution)/shard_map/sub | solution.py:29
  150.5 6.0 %copy.14 = f32[16,16384]{1,0:T(8,128)} copy(f32[16,16384]{0,1:T(8,128)} %divide_subtract_fusion) | data formatting | bytes 2097152
  (2 shorter events, 0.0 us)
Async XLA Ops:
  7.2 44.4 %all-to-all-start = ((bf16[16,16,128]{2,1,0:T(8,128)(2,1)}), bf16[16,16,128]{2,1,0:T(8,128)(2,1)S(1)}, u32[]{:S(2)}, u32[]{:S(2)}) async-start(bf16[16,16,128]{2,1,0:T(8,128)(2,1)} %bitcast.12), calls=%async_computation | async-start | bytes 131072 | tf_op jit(solution)/shard_map/all_to_all | solution.py:19
  13.4 121.5 %all-gather.4.cloned.1.call-start = ((), (), s32[]{:S(2)}) async-start(), calls=%async_computation.1 | async-start | bytes 1114112 | tf_op jit(solution)/shard_map/all_gather | solution.py:27
  66.7 31.4 %copy-start = (f32[16,16384]{1,0:T(8,128)S(1)}, f32[16,16384]{1,0:T(8,128)}, u32[]{:S(2)}) copy-start(f32[16,16384]{1,0:T(8,128)} %param.6) | copy-start | bytes 3145732
  98.0 38.5 %copy-start.1 = (f32[16384]{0:T(1024)S(1)}, f32[16384]{0:T(1024)}, u32[]{:S(2)}) copy-start(f32[16384]{0:T(1024)} %param.7) | copy-start | bytes 196612
Sparse Core Ops, SparseCore 0:
  98.2 36.7 all-gather.3

commit v2 on v0

--- a/solution.py
+++ b/solution.py
@@ -5,6 +5,12 @@
 
 W = 256
 learn_rate = 0.5
+
+
+def gathered_along(shard, name, along):
+    blocks = lax.all_gather(shard, name, axis=0, tiled=False)
+    result = jnp.concatenate(blocks, axis=along)
+    return result
 
 
 def accumulate(grads, ids, first_row, count_rows):
@@ -20,9 +26,7 @@
     local_rows = table_block.shape[1]
     all_row_ids = lax.all_gather(row_ids, ("dp", "table"), axis=0, tiled=True)
     first_row = lax.axis_index("dp") * local_rows
-    row_grad = accumulate(
-        lax.all_gather(owned, "dp", axis=1, tiled=True), all_row_ids, first_row, local_rows
-    )
+    row_grad = accumulate(gathered_along(owned, "dp", 1), all_row_ids, first_row, local_rows)
     partial_squares = jnp.sum(row_grad * row_grad, axis=0)
     squares = lax.psum(partial_squares, "table")
     new_state = adagrad_state + squares / W

time: 215 us -> 205 us (0.953)
  blocking collectives: 52.9 us -> 43 us
    all_gather x1, blocking collectives: 14.8 us -> 5 us  [gathered_along(): blocks = lax.all_gather(shard, name, axis=0, tiled=False)]
where the time goes in v2:
time: 205 us
  waiting for transfers between devices  84.2 us (41%)
  other arithmetic  46.1 us (22%)
  blocking collectives  43 us (21%)
  between operations  14.1 us (7%)
  local copies, waits for them, and re-layouts  11.3 us (6%)
  starting transfers between devices  6.32 us (3%)
    psum x1, waiting for transfers between devices, body(): squares = lax.psum(partial_squares, 'table')  84.2 us
    all_gather x1, blocking collectives, body(): all_row_ids = lax.all_gather(row_ids, ('dp', 'table'), axis=0, tiled=True)  38 us
    scatter-add x1, other arithmetic, accumulate(): return start_total.at[:, target].add(grads.astype(jnp.float32), mode='drop')  26.1 us
    sub x1, other arithmetic, body(): table_block - learn_rate * row_grad / jnp.sqrt(new_state)[None, :]  13.3 us
    unnamed x6, local copies, waits for them, and re-layouts  10.6 us
    all_to_all x1, starting transfers between devices, body(): lax.all_to_all(gradients, 'table', split_axis=0, concat_axis=1, tiled=True)  6.28 us
    reduce_sum x1, other arithmetic, body(): partial_squares = jnp.sum(row_grad * row_grad, axis=0)  5.28 us
    all_gather x1, blocking collectives, gathered_along(): blocks = lax.all_gather(shard, name, axis=0, tiled=False)  5 us
  transfers between devices with their start and end apart: 2, of which 1 were waited for; matrix products, arithmetic and copies ran while one was open for 2% of the time, Pallas kernels for 0%

profile of v2, /device:TPU:8, one launch (start us, length us, event | category | flops | bytes accessed | tf_op | source)
XLA Modules:
  0.0 205.1 jit_solution(8947581150993282259)
XLA Ops:
  7.2 6.3 %all-to-all-start = ((bf16[16,16,128]{2,1,0:T(8,128)(2,1)}), bf16[16,16,128]{2,1,0:T(8,128)(2,1)S(1)}, u32[]{:S(2)}, u32[]{:S(2)}) async-start(bf16[16,16,128]{2,1,0:T(8,128)(2,1)} %bitcast.14), calls=%async_computation | async-start | bytes 131072 | tf_op jit(solution)/shard_map/all_to_all | solution.py:25
  13.4 0.0 all-reduce.2.cloned.1.call-start
  13.5 38.0 %all-gather = s32[32,1,128]{2,1,0:T(1,128)S(1)} all-gather(s32[1,1,128]{2,1,0:T(1,128)} %bitcast.17), channel_id=1, replica_groups=mesh['dp'=2,'table'=16] {'dp','table'}, dimensions={0}, use_global_device_ids=true | all-gather | bytes 16896 | tf_op jit(solution)/shard_map/all_gather | solution.py:27
  51.5 0.0 all-to-all-done
  51.6 5.0 %all_gather.11 = bf16[2,16,2048]{2,1,0:T(8,128)(2,1)S(1)} all-gather(bf16[1,16,2048]{2,1,0:T(8,128)(2,1)S(1)} %all_gather.10), channel_id=1, replica_groups=mesh['dp'=2,'table'=16] {'dp'}, dimensions={0}, use_global_device_ids=true | all-gather | bytes 196608 | tf_op jit(solution)/shard_map/all_gather | solution.py:11
  56.7 0.6 copy.18
  57.3 0.0 copy-start
  57.3 26.1 %scatter_custom_fusion = f32[16,16384]{0,1:T(8,128)} fusion(s32[4096]{0:T(1024)S(1)} %compare_select_fusion, f32[4096,16]{1,0:T(8,128)S(1)} %copy.18, f32[]{:T(128)} %constant.7.clone.1), kind=kCustom, calls=%fused_computation.3 | custom fusion | flops 65536 | bytes 1048580 | tf_op jit(solution)/shard_map/scatter-add | solution.py:21
  83.3 0.0 copy-start.1
  83.4 5.3 %multiply_reduce_fusion = f32[16384]{0:T(1024)} fusion(f32[16,16384]{0,1:T(8,128)} %scatter_custom_fusion), kind=kLoop, calls=%fused_computation.2 | loop fusion | flops 507904 | bytes 1114112 | tf_op jit(solution)/shard_map/reduce_sum | solution.py:30
  88.6 0.0 all-reduce.2.cloned.1.call-update
  88.7 0.0 copy-done
  88.7 4.6 %copy.19 = f32[16,16384]{0,1:T(8,128)} copy(f32[16,16384]{1,0:T(8,128)S(1)} %copy-done) | data formatting | bytes 2097152 | tf_op args[2]
  93.3 84.2 %all-reduce.2.cloned.1.call-done = f32[16384]{0:T(1024)} async-done(((f32[16384]{0:T(1024)}), f32[16384]{0:T(1024)}) %all-reduce.2.cloned.1.call-update) | async-done | bytes 65552 | tf_op jit(solution)/shard_map/psum | solution.py:31
  177.5 0.0 copy-done.1
  177.5 1.5 fusion.2
  179.0 13.3 %divide_subtract_fusion = f32[16,16384]{0,1:T(8,128)} fusion(f32[16,16384]{0,1:T(8,128)} %copy.19, f32[16,16384]{0,1:T(8,128)} %scatter_custom_fusion, f32[16384]{0:T(1024)S(1)} %get-tuple-element.10), kind=kLoop, calls=%fused_computation.1 | loop fusion | flops 786432 | bytes 3211264 | tf_op jit(solution)/shard_map/sub | solution.py:33
  192.2 6.0 %copy.20 = f32[16,16384]{1,0:T(8,128)} copy(f32[16,16384]{0,1:T(8,128)} %divide_subtract_fusion) | data formatting | bytes 2097152
  (6 shorter events, 0.1 us)
Async XLA Ops:
  7.2 44.4 %all-to-all-start = ((bf16[16,16,128]{2,1,0:T(8,128)(2,1)}), bf16[16,16,128]{2,1,0:T(8,128)(2,1)S(1)}, u32[]{:S(2)}, u32[]{:S(2)}) async-start(bf16[16,16,128]{2,1,0:T(8,128)(2,1)} %bitcast.14), calls=%async_computation | async-start | bytes 131072 | tf_op jit(solution)/shard_map/all_to_all | solution.py:25
  13.4 164.0 %all-reduce.2.cloned.1.call-start = ((), (), s32[]{:S(2)}) async-start(), calls=%async_computation.1 | async-start | bytes 131072 | tf_op jit(solution)/shard_map/psum | solution.py:31
  57.3 31.4 %copy-start = (f32[16,16384]{1,0:T(8,128)S(1)}, f32[16,16384]{1,0:T(8,128)}, u32[]{:S(2)}) copy-start(f32[16,16384]{1,0:T(8,128)} %param.6) | copy-start | bytes 3145732
  83.3 94.1 %copy-start.1 = (f32[16384]{0:T(1024)S(1)}, f32[16384]{0:T(1024)}, u32[]{:S(2)}) copy-start(f32[16384]{0:T(1024)} %param.7) | copy-start | bytes 196612
Sparse Core Ops, SparseCore 0:
  88.8 88.6 all-reduce.1
